TPU v7x, 128 devices: a whole 4x4x4 slice. The times are simulated.
128 devices in a mesh: seq: 16 (over z, y), tensor: 8 (over x, core).
Axes of the slice: x: 4, y: 4, z: 4, core: 2. Of those that a mesh axis runs over, the one named last changes fastest.
Arguments:
- tokens: bfloat16 [256, 4, 3072], P('seq'), may hold values from -6 to 6
- lengths: int32 [256], replicated, may hold values from 1 to 16384, as said below
- page_request: int32 [2048], P('seq'), may hold values from 0 to 255, as said below
- page_block: int32 [2048], P('seq'), may hold values from 0 to 128, as said below
- k_cache: bfloat16 [2048, 8, 128, 128], P('seq', 'tensor'), may hold values from -330 to 330
- v_cache: bfloat16 [2048, 8, 128, 128], P('seq', 'tensor'), may hold values from -6 to 6
- attn_gain: bfloat16 [3072], replicated, may hold values from 0.099609375 to 1.8984375
- w_query: bfloat16 [3072, 3072], P(None, 'tensor'), may hold values from -0.109375 to 0.109375
- w_key: bfloat16 [3072, 1024], P(None, 'tensor'), may hold values from -0.109375 to 0.109375
- w_value: bfloat16 [3072, 1024], P(None, 'tensor'), may hold values from -0.109375 to 0.109375
- w_out: bfloat16 [3072, 3072], P('tensor'), may hold values from -0.109375 to 0.109375
- mlp_gain: bfloat16 [3072], replicated, may hold values from 0.099609375 to 1.8984375
- w_gate: bfloat16 [3072, 4096], P(None, 'tensor'), may hold values from -0.109375 to 0.109375
- w_up: bfloat16 [3072, 4096], P(None, 'tensor'), may hold values from -0.109375 to 0.109375
- w_down: bfloat16 [4096, 3072], P('tensor'), may hold values from -0.09375 to 0.09375
Outputs:
- layer_out: bfloat16 [256, 4, 3072], P('seq', None, 'tensor')
Inputs may be any that keep to these rules, and one draw needn't show every extreme that they name: `lengths`: A request r whose index is a multiple of 32 has a long cache, within 128 tokens of 16384; the others have at most 511. Request 0 has exactly 16384. `page_request`: each pair of a long request and a page number below 128, or of a short request and a page number below 4, appears in exactly one slot; slots of pages at or beyond a request's length hold no used position. A short request's pages lie in the slots of the seq index that holds its tokens. `page_block`: slots of page number 128 hold no used position.
All inputs are finite; a program needn't handle non-finite values.
Results may differ from a plain program's by a relative error of at most 0.012.
Values may be sent and summed in bfloat16 or wider, within the bound.
No kernel may reach another device: no remote copies, remote signals or barrier semaphores. Data moves between devices by JAX's collectives and lax.ppermute only.
A program may use at most 128 MiB of HBM per device.

v0:
```python
import math
import jax
import jax.numpy as jnp
from jax import lax
from jax.sharding import PartitionSpec as P

EPSILON = 1e-05
NEGATIVE = -1e30
ROPE_BASE = 500000.0


def rms_norm(values, gains):
    mean_square = jnp.mean(values * values, axis=-1, keepdims=True)
    return values * lax.rsqrt(mean_square + EPSILON) * gains.astype(jnp.float32)


def rotary(values, position):
    head_width = values.shape[-1]
    half_width = head_width // 2
    inverse = 1.0 / ROPE_BASE ** (jnp.arange(half_width, dtype=jnp.float32) * 2.0 / head_width)
    angle = position.astype(jnp.float32)[..., None, None] * inverse
    cosine = jnp.cos(angle)
    sine_table = jnp.sin(angle)
    front_half = values[..., :half_width]
    back_half = values[..., half_width:]
    return jnp.concatenate(
        [
            front_half * cosine - back_half * sine_table,
            back_half * cosine + front_half * sine_table,
        ],
        axis=-1,
    )


def per_device(
    tokens,
    lengths,
    page_request,
    page_block,
    k_cache,
    v_cache,
    attn_gain,
    w_query,
    w_key,
    w_value,
    w_out,
    mlp_gain,
    w_gate,
    w_up,
    w_down,
):
    req_dev, fresh_count, model_width = tokens.shape
    head_dim = k_cache.shape[-1]
    page_len = k_cache.shape[2]
    kv_local = k_cache.shape[1]
    group_size = w_query.shape[1] // (kv_local * head_dim)
    lanes = fresh_count * group_size
    row_count = req_dev * fresh_count
    score_scale = 1.0 / math.sqrt(head_dim)
    seq_index = lax.axis_index("seq")
    home_row = seq_index * req_dev
    own_length = lax.dynamic_slice_in_dim(lengths, home_row, req_dev)
    position = own_length[:, None] + jnp.arange(fresh_count, dtype=jnp.int32)[None, :]
    values_in = tokens.astype(jnp.float32)
    normed_in = rms_norm(values_in, attn_gain).astype(jnp.bfloat16).reshape(row_count, model_width)
    queries = jnp.dot(normed_in, w_query, preferred_element_type=jnp.float32).reshape(
        req_dev, fresh_count, kv_local * group_size, head_dim
    )
    queries = rotary(queries, position).astype(jnp.bfloat16)
    queries = queries.reshape(req_dev, fresh_count, kv_local, group_size, head_dim).transpose(
        0, 2, 1, 3, 4
    )
    queries = queries.reshape(req_dev, kv_local, lanes, head_dim)
    key_new = jnp.dot(normed_in, w_key, preferred_element_type=jnp.float32).reshape(
        req_dev, fresh_count, kv_local, head_dim
    )
    key_new = rotary(key_new, position).astype(jnp.bfloat16).transpose(0, 2, 1, 3)
    value_new = jnp.dot(normed_in, w_value, preferred_element_type=jnp.float32).astype(jnp.bfloat16)
    value_new = value_new.reshape(req_dev, fresh_count, kv_local, head_dim).transpose(0, 2, 1, 3)
    requests = lengths.shape[0]
    owner_member = page_request[:, None] == jnp.arange(requests, dtype=jnp.int32)[None, :]
    owner_length = jnp.sum(jnp.where(owner_member, lengths[None, :], 0), axis=1)
    offsets = jnp.arange(page_len, dtype=jnp.int32)
    is_valid = page_block[:, None] * page_len + offsets[None, :] < owner_length[:, None]
    fresh_scores = (
        jnp.einsum("rhqd,rhsd->rhqs", queries, key_new, preferred_element_type=jnp.float32)
        * score_scale
    )
    causal = (jnp.arange(lanes, dtype=jnp.int32) // group_size)[:, None] >= jnp.arange(
        fresh_count, dtype=jnp.int32
    )[None, :]
    fresh_scores = jnp.where(causal[None, None], fresh_scores, NEGATIVE)
    fresh_top = jnp.max(fresh_scores, axis=-1)
    every_query = lax.all_gather(
        queries.reshape(req_dev, kv_local * lanes * head_dim), "seq", axis=0, tiled=True
    )
    chosen = every_query[page_request].reshape(-1, kv_local, lanes, head_dim)
    scores = (
        jnp.einsum("phqd,phkd->phqk", chosen, k_cache, preferred_element_type=jnp.float32)
        * score_scale
    )
    scores = jnp.where(is_valid[:, None, None, :], scores, NEGATIVE)
    page_max = jnp.max(scores, axis=-1)
    cache_max = jnp.max(
        jnp.where(owner_member[:, :, None, None], page_max[:, None], NEGATIVE), axis=0
    )
    own_max = jnp.maximum(lax.dynamic_slice_in_dim(cache_max, home_row, req_dev, 0), fresh_top)
    candidate = lax.dynamic_update_slice_in_dim(cache_max, own_max, home_row, 0)
    row_max = lax.pmax(candidate, "seq")
    page_ref = jnp.sum(jnp.where(owner_member[:, :, None, None], row_max[None], 0.0), axis=1)
    weights = jnp.where(
        is_valid[:, None, None, :], jnp.exp(scores - page_ref[..., None]), 0.0
    ).astype(jnp.bfloat16)
    page_total = jnp.sum(weights.astype(jnp.float32), axis=-1)
    page_sum = jnp.einsum("phqk,phkd->phqd", weights, v_cache, preferred_element_type=jnp.float32)
    member_float = owner_member.astype(jnp.float32)
    slot_total = jnp.einsum(
        "pr,phq->rhq", member_float, page_total, precision=lax.Precision.HIGHEST
    )
    slot_summed = jnp.einsum(
        "pr,phqd->rhqd", member_float, page_sum, precision=lax.Precision.HIGHEST
    )
    total_all, summed_all = lax.psum((slot_total, slot_summed), "seq")
    own_total = lax.dynamic_slice_in_dim(total_all, home_row, req_dev, 0)
    own_summed = lax.dynamic_slice_in_dim(summed_all, home_row, req_dev, 0)
    own_ref = lax.dynamic_slice_in_dim(row_max, home_row, req_dev, 0)
    fresh_weights = jnp.where(
        causal[None, None], jnp.exp(fresh_scores - own_ref[..., None]), 0.0
    ).astype(jnp.bfloat16)
    own_total = own_total + jnp.sum(fresh_weights.astype(jnp.float32), axis=-1)
    own_summed = own_summed + jnp.einsum(
        "rhqs,rhsd->rhqd", fresh_weights, value_new, preferred_element_type=jnp.float32
    )
    attended = (own_summed / own_total[..., None]).astype(jnp.bfloat16)
    attended = attended.reshape(req_dev, kv_local, fresh_count, group_size, head_dim).transpose(
        0, 2, 1, 3, 4
    )
    attended = attended.reshape(row_count, kv_local * group_size * head_dim)
    partial_value = jnp.dot(attended, w_out, preferred_element_type=jnp.float32)
    flat_input = values_in.reshape(row_count, model_width)
    col_count = model_width // lax.axis_size("tensor")
    col_start = lax.axis_index("tensor") * col_count
    attn_sum = lax.psum(partial_value, "tensor")
    residual = (flat_input + attn_sum).astype(jnp.bfloat16)
    normed = rms_norm(residual.astype(jnp.float32), mlp_gain).astype(jnp.bfloat16)
    own_residual = lax.dynamic_slice_in_dim(residual, col_start, col_count, 1)
    gate_out = jnp.dot(normed, w_gate, preferred_element_type=jnp.float32)
    up_out = jnp.dot(normed, w_up, preferred_element_type=jnp.float32)
    activated = (jax.nn.silu(gate_out) * up_out).astype(jnp.bfloat16)
    down_out = jnp.dot(activated, w_down, preferred_element_type=jnp.float32)
    mlp_part = lax.psum_scatter(down_out, "tensor", scatter_dimension=1, tiled=True)
    layer_out = (own_residual.astype(jnp.float32) + mlp_part).astype(jnp.bfloat16)
    return layer_out.reshape(req_dev, fresh_count, col_count)


def solution(mesh):
    placed = (
        P("seq", None, None),
        P(),
        P("seq"),
        P("seq"),
        P("seq", "tensor", None, None),
        P("seq", "tensor", None, None),
        P(),
        P(None, "tensor"),
        P(None, "tensor"),
        P(None, "tensor"),
        P("tensor", None),
        P(),
        P(None, "tensor"),
        P(None, "tensor"),
        P("tensor", None),
    )
    return jax.shard_map(
        per_device, mesh=mesh, in_specs=placed, out_specs=P("seq", None, "tensor"), check_vma=False
    )
```

profile of v0, /device:TPU:0, one launch (start us, length us, event | category | flops | bytes accessed | tf_op | source)
XLA Modules:
  0.0 368.0 jit_solution(6125877273214239145)
XLA Ops:
  6.6 1.4 multiply_reduce_fusion
  10.0 2.0 fusion.69
  17.1 1.4 convolution_bitcast_fusion.1
  20.7 4.3 %copy.81 = bf16[3072,384]{0,1:T(8,128)(2,1)} copy(bf16[3072,384]{1,0:T(8,128)(2,1)} %param.22) | data formatting | bytes 4718592 | tf_op args[7]
  25.0 2.7 fusion.18
  30.2 1.5 copy.83
  31.6 1.5 convert_element_type.77
  33.1 28.5 %all_gather.3 = bf16[256,1536]{1,0:T(8,128)(2,1)} all-gather(bf16[16,1536]{1,0:T(8,128)(2,1)} %convert_element_type.77), channel_id=1, replica_groups=mesh['seq'=16,'tensor'=8] {'seq'}, dimensions={0}, use_global_device_ids=true | all-gather | bytes 835584 | tf_op jit(solution)/shard_map/all_gather | solution.py:94
  62.3 3.2 gather_fusion
  65.5 1.9 copy.84
  67.4 2.2 copy.85
  70.4 6.3 %fusion.55 = (f32[128,12]{1,0:T(8,128)}, f32[128,12,128]{2,1,0:T(8,128)}) fusion(bf16[128,12,128]{2,1,0:T(8,128)(2,1)} %copy.85, bf16[128,1,128,128]{3,2,1,0:T(8,128)(2,1)} %param.19, pred[128,128]{1,0:T(8,128)(4,1)S(1)} %add_compare_fusion), kind=kOutput, calls=%fused_computation.94 | convolution fusion | flops 50919936 | bytes 5396480 | tf_op jit(solution)/shard_map/phqd,phkd->phqk/dot_general | solution.py:99
  76.6 1.5 copy.87
  78.2 1.5 copy.86
  84.0 72.1 %pmax.7 = f32[256,1,12]{0,2,1:T(8,128)} all-reduce(f32[256,1,12]{0,2,1:T(8,128)} %dynamic_update_slice.3), channel_id=1, replica_groups=mesh['seq'=16,'tensor'=8] {'seq'}, use_global_device_ids=true, to_apply=%region_5.6 | all-reduce | flops 3072 | bytes 24576 | tf_op jit(solution)/shard_map/pmax | solution.py:109
  156.1 1.7 select_reduce_fusion
  159.2 3.8 %fusion = f32[128,12,128]{2,1,0:T(8,128)S(1)} fusion(bf16[128,1,128,128]{3,2,1,0:T(8,128)(2,1)} %param.20, f32[128,12,128]{2,1,0:T(8,128)} %get-tuple-element.14, f32[128,12]{1,0:T(8,128)} %copy.93, pred[128,128]{1,0:T(8,128)(4,1)S(1)} %add_compare_fusion), kind=kOutput, calls=%fused_computation.1 | convolution fusion | flops 50921472 | bytes 5789696 | tf_op jit(solution)/shard_map/phqk,phkd->phqd/dot_general | solution.py:115
  163.0 2.2 convolution_bitcast_fusion
  168.4 1.9 convert_reduce_fusion
  171.2 69.6 %psum.22 = f32[256,1,12]{0,2,1:T(8,128)} all-reduce(f32[256,1,12]{0,2,1:T(8,128)S(1)} %convolution_bitcast_fusion.2), channel_id=1, replica_groups=mesh['seq'=16,'tensor'=8] {'seq'}, use_global_device_ids=true, to_apply=%region_9.10 | all-reduce | flops 3072 | bytes 24576 | tf_op jit(solution)/shard_map/psum | solution.py:123
  241.6 1.5 convolution_convert_fusion
  243.1 1.6 fusion.54
  244.8 5.9 %all-reduce.3.cloned.1.call-done = f32[256,1,12,128]{3,0,2,1:T(8,128)} async-done(((f32[256,1,12,128]{3,0,2,1:T(8,128)}), f32[256,1,12,128]{3,0,2,1:T(8,128)}) %all-reduce.3.cloned.1.call-update) | async-done | bytes 1572880 | tf_op jit(solution)/shard_map/psum | solution.py:123
  252.4 1.5 reshape_transpose_reshape.4
  253.9 3.1 fusion.57
  258.7 59.7 %all-reduce.5.cloned.1.call-done = f32[64,3072]{1,0:T(8,128)} async-done(((f32[64,3072]{1,0:T(8,128)}), f32[64,3072]{1,0:T(8,128)}) %all-reduce.5.cloned.1.call-update) | async-done | bytes 786448 | tf_op jit(solution)/shard_map/psum | solution.py:143
  318.5 1.6 fusion.13
  320.1 3.3 fusion.29
  323.3 4.1 %fusion.11 = f32[64,3072]{1,0:T(8,128)} fusion(bf16[512,3072]{1,0:T(8,128)(2,1)S(1)} %copy-done, bf16[3072,512]{1,0:T(8,128)(2,1)} %param.28, f32[64,512]{1,0:T(8,128)} %fusion.29, bf16[64,3072]{1,0:T(8,128)(2,1)S(1)} %get-tuple-element.6, f32[3072]{0:T(1024)S(1)} %convert_element_type.87, f32[64]{0:T(128)S(1)} %add_rsqrt_fusion.1), kind=kOutput, calls=%fused_computation.12 | convolution fusion | flops 403636224 | bytes 7614720 | tf_op jit(solution)/shard_map/dot_general | solution.py:150
  327.4 31.1 %reduce-scatter.2.cloned.1.call-done = f32[64,384]{1,0:T(8,128)} async-done(((f32[64,3072]{1,0:T(8,128)}), f32[64,384]{1,0:T(8,128)}) %reduce-scatter.2.cloned.1.call-update) | async-done | bytes 98320 | tf_op jit(solution)/shard_map/reduce_scatter | solution.py:151
  358.5 1.5 add_convert_fusion.1
  360.1 1.4 reshape.282
  (69 shorter events, 27.2 us)
Async XLA Ops:
  6.5 316.8 %copy-start = (bf16[512,3072]{1,0:T(8,128)(2,1)S(1)}, bf16[512,3072]{1,0:T(8,128)(2,1)}, u32[]{:S(2)}) copy-start(bf16[512,3072]{1,0:T(8,128)(2,1)} %param.29) | copy-start | bytes 9437188
  6.5 244.1 %all-reduce.3.cloned.1.call-start = ((), (), s32[]{:S(2)}) async-start(), calls=%async_computation.1 | async-start | bytes 3145728 | tf_op jit(solution)/shard_map/psum | solution.py:123
  6.6 12.0 %copy-start.9 = (f32[64]{0:T(128)}, f32[64]{0:T(128)S(1)}, u32[]{:S(2)}) copy-start(f32[64]{0:T(128)S(1)} %negate_power_fusion) | copy-start | bytes 772
  25.0 2.7 copy-start.2
  25.0 2.7 copy-start.3
  25.0 3.6 copy-start.11
  25.0 3.6 copy-start.6
  28.6 0.9 copy-start.8
  30.2 39.4 %copy-start.10 = (s32[128]{0:T(128)S(1)}, s32[128]{0:T(128)}, u32[]{:S(2)}) copy-start(s32[128]{0:T(128)} %param.18) | copy-start | bytes 1540
  80.7 0.6 copy-start.4
  159.2 3.8 %copy-start.7 = (s32[128]{0:T(128)S(1)}, s32[128]{0:T(128)}, u32[]{:S(2)}) copy-start(s32[128]{0:T(128)} %param.17) | copy-start | bytes 1540
  165.2 153.3 %all-reduce.5.cloned.1.call-start = ((), (), s32[]{:S(2)}) async-start(), calls=%async_computation.2 | async-start | bytes 1572864 | tf_op jit(solution)/shard_map/psum | solution.py:143
  166.9 1.5 copy-start.5
  170.3 86.8 %copy-start.1 = (bf16[16,4,3072]{2,1,0:T(4,128)(2,1)S(1)}, bf16[16,4,3072]{2,1,0:T(4,128)(2,1)}, u32[]{:S(2)}) copy-start(bf16[16,4,3072]{2,1,0:T(4,128)(2,1)} %param.15) | copy-start | bytes 1179652
  257.0 101.5 %reduce-scatter.2.cloned.1.call-start = ((), (), s32[]{:S(2)}) async-start(), calls=%async_computation.3 | async-start | bytes 884736 | tf_op jit(solution)/shard_map/reduce_scatter | solution.py:151
Sparse Core Ops, SparseCore 0:
  165.3 85.3 all-reduce.2
  257.1 61.2 all-reduce.4
  327.6 30.9 reduce-scatter.1
where the time goes:
time: 370 us; the launch traced here: 368 us
  blocking collectives  170 us (46%)
  waiting for transfers between devices  96.8 us (26%)
  matrix products  31.7 us (9%)
  local copies, waits for them, and re-layouts  29.3 us (8%)
  other arithmetic  26.6 us (7%)
  between operations  13.3 us (4%)
    pmax x1, blocking collectives, per_device(): row_max = lax.pmax(candidate, 'seq')  72.1 us
    psum x1, blocking collectives, per_device(): total_all, summed_all = lax.psum((slot_total, slot_summed), 'seq')  69.6 us
    psum x1, waiting for transfers between devices, per_device(): attn_sum = lax.psum(partial_value, 'tensor')  59.7 us
    reduce_scatter x1, waiting for transfers between devices, per_device(): lax.psum_scatter(down_out, 'tensor', scatter_dimension=1, tiled=True)  31.1 us
    all_gather x1, blocking collectives, per_device(): lax.all_gather(queries.reshape(req_dev, kv_local * lanes * head_dim), 'se...  28.5 us
  transfers between devices with their start and end apart: 3, of which 3 were waited for; matrix products, arithmetic and copies ran while one was open for 3% of the time, Pallas kernels for 0%

commit v1 on v0

--- a/solution.py
+++ b/solution.py
@@ -140,7 +140,11 @@
     flat_input = values_in.reshape(row_count, model_width)
     col_count = model_width // lax.axis_size("tensor")
     col_start = lax.axis_index("tensor") * col_count
-    attn_sum = lax.psum(partial_value, "tensor")
+    attn_sum = partial_value
+    for hop in (1, 2, 4):
+        attn_sum = attn_sum + lax.ppermute(
+            attn_sum, "tensor", [(dev, dev ^ hop) for dev in range(8)]
+        )
     residual = (flat_input + attn_sum).astype(jnp.bfloat16)
     normed = rms_norm(residual.astype(jnp.float32), mlp_gain).astype(jnp.bfloat16)
     own_residual = lax.dynamic_slice_in_dim(residual, col_start, col_count, 1)

time: 370 us -> 350 us (0.946)
  waiting for transfers between devices: 96.8 us -> 75.4 us
  starting transfers between devices: 0.09 us -> 4.86 us
    psum x1 -> x0, waiting for transfers between devices: 59.7 us -> none  [per_device(): attn_sum = lax.psum(partial_value, 'tensor')]
    ppermute x0 -> x3, waiting for transfers between devices: none -> 36.1 us  [per_device(): lax.ppermute(attn_sum, 'tensor', [(dev, dev ^ hop) for dev in range(8)])]
    ppermute x0 -> x3, starting transfers between devices: none -> 4.81 us  [per_device(): lax.ppermute(attn_sum, 'tensor', [(dev, dev ^ hop) for dev in range(8)])]
  transfers between devices with their start and end apart: 3 -> 5, of which waited for: 3 -> 5; matrix products, arithmetic and copies ran while one was open for 3% -> 3% of each run, Pallas kernels for 0% -> 0%
where the time goes in v1:
time: 350 us; the launch traced here: 348 us
  blocking collectives  170 us (49%)
  waiting for transfers between devices  75.4 us (22%)
  matrix products  30.1 us (9%)
  other arithmetic  27.1 us (8%)
  local copies, waits for them, and re-layouts  26.6 us (8%)
  between operations  13.6 us (4%)
  starting transfers between devices  4.86 us (1%)
    pmax x1, blocking collectives, per_device(): row_max = lax.pmax(candidate, 'seq')  72.1 us
    psum x1, blocking collectives, per_device(): total_all, summed_all = lax.psum((slot_total, slot_summed), 'seq')  69.7 us
    ppermute x3, waiting for transfers between devices, per_device(): lax.ppermute(attn_sum, 'tensor', [(dev, dev ^ hop) for dev in range(8)])  36.1 us
    reduce_scatter x1, waiting for transfers between devices, per_device(): lax.psum_scatter(down_out, 'tensor', scatter_dimension=1, tiled=True)  31.3 us
    all_gather x1, blocking collectives, per_device(): lax.all_gather(queries.reshape(req_dev, kv_local * lanes * head_dim), 'se...  28.5 us
    psum x1, waiting for transfers between devices, per_device(): total_all, summed_all = lax.psum((slot_total, slot_summed), 'seq')  7.94 us
  transfers between devices with their start and end apart: 5, of which 5 were waited for; matrix products, arithmetic and copies ran while one was open for 3% of the time, Pallas kernels for 0%

profile of v1, /device:TPU:0, one launch (start us, length us, event | category | flops | bytes accessed | tf_op | source)
XLA Modules:
  0.0 348.0 jit_solution(10527965106581002200)
XLA Ops:
  10.0 2.0 fusion.69
  17.0 1.4 convolution_bitcast_fusion.1
  20.7 4.3 %copy.81 = bf16[3072,384]{0,1:T(8,128)(2,1)} copy(bf16[3072,384]{1,0:T(8,128)(2,1)} %param.22) | data formatting | bytes 4718592 | tf_op args[7]
  25.0 2.7 fusion.18
  30.2 1.5 copy.83
  31.6 1.5 convert_element_type.77
  33.1 28.5 %all_gather.3 = bf16[256,1536]{1,0:T(8,128)(2,1)} all-gather(bf16[16,1536]{1,0:T(8,128)(2,1)} %convert_element_type.77), channel_id=1, replica_groups=mesh['seq'=16,'tensor'=8] {'seq'}, dimensions={0}, use_global_device_ids=true | all-gather | bytes 835584 | tf_op jit(solution)/shard_map/all_gather | solution.py:94
  62.3 3.2 gather_fusion
  65.5 1.9 copy.84
  67.4 2.2 copy.85
  70.4 6.3 %fusion.55 = (f32[128,12]{1,0:T(8,128)}, f32[128,12,128]{2,1,0:T(8,128)}) fusion(bf16[128,12,128]{2,1,0:T(8,128)(2,1)} %copy.85, bf16[128,1,128,128]{3,2,1,0:T(8,128)(2,1)} %param.19, pred[128,128]{1,0:T(8,128)(4,1)S(1)} %add_compare_fusion), kind=kOutput, calls=%fused_computation.94 | convolution fusion | flops 50919936 | bytes 5396480 | tf_op jit(solution)/shard_map/phqd,phkd->phqk/dot_general | solution.py:99
  76.7 1.5 copy.87
  78.2 1.5 copy.86
  84.0 72.1 %pmax.7 = f32[256,1,12]{0,2,1:T(8,128)} all-reduce(f32[256,1,12]{0,2,1:T(8,128)} %dynamic_update_slice.3), channel_id=1, replica_groups=mesh['seq'=16,'tensor'=8] {'seq'}, use_global_device_ids=true, to_apply=%region_5.6 | all-reduce | flops 3072 | bytes 24576 | tf_op jit(solution)/shard_map/pmax | solution.py:109
  156.1 1.7 select_reduce_fusion
  159.2 3.8 %fusion = f32[128,12,128]{2,1,0:T(8,128)S(1)} fusion(bf16[128,1,128,128]{3,2,1,0:T(8,128)(2,1)} %param.20, f32[128,12,128]{2,1,0:T(8,128)} %get-tuple-element.14, f32[128,12]{1,0:T(8,128)} %copy.93, pred[128,128]{1,0:T(8,128)(4,1)S(1)} %add_compare_fusion), kind=kOutput, calls=%fused_computation.1 | convolution fusion | flops 50921472 | bytes 5789696 | tf_op jit(solution)/shard_map/phqk,phkd->phqd/dot_general | solution.py:115
  163.0 2.2 convolution_bitcast_fusion
  167.8 1.9 convert_reduce_fusion
  170.6 69.7 %psum.15 = f32[256,1,12]{0,2,1:T(8,128)S(1)} all-reduce(f32[256,1,12]{0,2,1:T(8,128)S(1)} %convolution_bitcast_fusion.2), channel_id=1, replica_groups=mesh['seq'=16,'tensor'=8] {'seq'}, use_global_device_ids=true, to_apply=%region_9.10 | all-reduce | flops 3072 | bytes 24576 | tf_op jit(solution)/shard_map/psum | solution.py:123
  240.3 1.5 convolution_convert_fusion
  242.8 7.9 %all-reduce.2.cloned.1.call-done = f32[256,1,12,128]{3,0,2,1:T(8,128)} async-done(((f32[256,1,12,128]{3,0,2,1:T(8,128)}), f32[256,1,12,128]{3,0,2,1:T(8,128)}) %all-reduce.2.cloned.1.call-update) | async-done | bytes 1572880 | tf_op jit(solution)/shard_map/psum | solution.py:123
  251.8 2.2 fusion.57
  254.1 2.3 collective-permute-done
  256.5 1.6 collective-permute-start.1
  258.1 18.0 %collective-permute-done.1 = f32[64,3072]{1,0:T(8,128)S(1)} collective-permute-done((f32[64,3072]{1,0:T(8,128)S(1)}, f32[64,3072]{1,0:T(8,128)S(1)}, u32[]{:S(2)}, u32[]{:S(2)}) %collective-permute-start.1) | collective-permute-done | bytes 786464 | tf_op jit(solution)/shard_map/ppermute | solution.py:145
  277.1 3.1 collective-permute-start.2
  281.8 15.8 %collective-permute-done.2 = f32[64,3072]{1,0:T(8,128)} collective-permute-done((f32[64,3072]{1,0:T(8,128)}, f32[64,3072]{1,0:T(8,128)}, u32[]{:S(2)}, u32[]{:S(2)}) %collective-permute-start.2) | collective-permute-done | bytes 786464 | tf_op jit(solution)/shard_map/ppermute | solution.py:145
  297.7 1.8 fusion.13
  299.5 3.3 fusion.29
  302.8 4.1 %fusion.11 = f32[64,3072]{1,0:T(8,128)} fusion(bf16[512,3072]{1,0:T(8,128)(2,1)S(1)} %copy-done, bf16[3072,512]{1,0:T(8,128)(2,1)} %param.28, f32[64,512]{1,0:T(8,128)} %fusion.29, bf16[64,3072]{1,0:T(8,128)(2,1)S(1)} %get-tuple-element.6, f32[3072]{0:T(1024)S(1)} %convert_element_type.87, f32[64]{0:T(128)S(1)} %add_rsqrt_fusion.1), kind=kOutput, calls=%fused_computation.12 | convolution fusion | flops 403636224 | bytes 7614720 | tf_op jit(solution)/shard_map/dot_general | solution.py:154
  306.9 31.3 %reduce-scatter.2.cloned.1.call-done = f32[64,384]{1,0:T(8,128)} async-done(((f32[64,3072]{1,0:T(8,128)}), f32[64,384]{1,0:T(8,128)}) %reduce-scatter.2.cloned.1.call-update) | async-done | bytes 98320 | tf_op jit(solution)/shard_map/reduce_scatter | solution.py:155
  338.2 1.5 add_convert_fusion.1
  (72 shorter events, 30.2 us)
Async XLA Ops:
  6.5 296.3 %copy-start = (bf16[512,3072]{1,0:T(8,128)(2,1)S(1)}, bf16[512,3072]{1,0:T(8,128)(2,1)}, u32[]{:S(2)}) copy-start(bf16[512,3072]{1,0:T(8,128)(2,1)} %param.29) | copy-start | bytes 9437188
  6.5 244.2 %all-reduce.2.cloned.1.call-start = ((), (), s32[]{:S(2)}) async-start(), calls=%async_computation.1 | async-start | bytes 3145728 | tf_op jit(solution)/shard_map/psum | solution.py:123
  6.6 11.9 %copy-start.8 = (f32[64]{0:T(128)}, f32[64]{0:T(128)S(1)}, u32[]{:S(2)}) copy-start(f32[64]{0:T(128)S(1)} %negate_power_fusion) | copy-start | bytes 772
  25.0 2.7 copy-start.2
  25.0 2.7 copy-start.3
  25.0 3.6 %copy-start.10 = (s32[12]{0:T(128)S(1)}, s32[12]{0:T(128)}, u32[]{:S(2)}) copy-start(s32[12]{0:T(128)} %and_select_fusion) | copy-start | bytes 148
  25.0 3.6 %copy-start.5 = (bf16[16,4,64]{2,0,1:T(8,128)(2,1)S(1)}, bf16[16,4,64]{2,0,1:T(8,128)(2,1)}, u32[]{:S(2)}) copy-start(bf16[16,4,64]{2,0,1:T(8,128)(2,1)} %get-tuple-element.10) | copy-start | bytes 24580
  28.6 0.9 copy-start.7
  30.2 39.4 %copy-start.9 = (s32[128]{0:T(128)S(1)}, s32[128]{0:T(128)}, u32[]{:S(2)}) copy-start(s32[128]{0:T(128)} %param.18) | copy-start | bytes 1540
  80.7 0.6 copy-start.4
  159.2 3.8 %copy-start.6 = (s32[128]{0:T(128)S(1)}, s32[128]{0:T(128)}, u32[]{:S(2)}) copy-start(s32[128]{0:T(128)} %param.17) | copy-start | bytes 1540
  165.2 173.0 %reduce-scatter.2.cloned.1.call-start = ((), (), s32[]{:S(2)}) async-start(), calls=%async_computation.2 | async-start | bytes 884736 | tf_op jit(solution)/shard_map/reduce_scatter | solution.py:155
  254.0 26.2 %copy-start.1 = (bf16[16,4,3072]{2,1,0:T(4,128)(2,1)S(1)}, bf16[16,4,3072]{2,1,0:T(4,128)(2,1)}, u32[]{:S(2)}) copy-start(bf16[16,4,3072]{2,1,0:T(4,128)(2,1)} %param.15) | copy-start | bytes 1179652
  254.0 2.4 collective-permute-start
  256.5 19.7 %collective-permute-start.1 = (f32[64,3072]{1,0:T(8,128)S(1)}, f32[64,3072]{1,0:T(8,128)S(1)}, u32[]{:S(2)}, u32[]{:S(2)}) collective-permute-start(f32[64,3072]{1,0:T(8,128)S(1)} %add.130), channel_id=1, source_target_pairs={{0,2},{1,3},{2,0},{3,1},{4,6},{5,7},{6,4},{7,5},{8,10},{9,11},{10,... | collective-permute-start | bytes 2359304 | tf_op jit(solution)/shard_map/ppermute | solution.py:145
  277.1 20.5 %collective-permute-start.2 = (f32[64,3072]{1,0:T(8,128)}, f32[64,3072]{1,0:T(8,128)}, u32[]{:S(2)}, u32[]{:S(2)}) collective-permute-start(f32[64,3072]{1,0:T(8,128)} %add.131), channel_id=1, source_target_pairs={{0,4},{1,5},{2,6},{3,7},{4,0},{5,1},{6,2},{7,3},{8,12},{9,13},{10,... | collective-permute-start | bytes 2359304 | tf_op jit(solution)/shard_map/ppermute | solution.py:145
Sparse Core Ops, SparseCore 0:
  165.3 85.3 all-reduce.1
  307.0 31.1 reduce-scatter.1
